TPU v7x, 32 devices: a whole 2x2x4 slice. The times are simulated.
32 devices in a mesh: shard: 8 (over z, y), tensor: 4 (over x, core).
Axes of the slice: x: 2, y: 2, z: 4, core: 2. Of those that a mesh axis runs over, the one named last changes fastest.
Arguments:
- acts: bfloat16 [2048, 1152], P('shard', 'tensor'), may hold values from -600 to 600
- outgrads: bfloat16 [2048, 1152], P('shard', 'tensor'), may hold values from -800 to 800
- weight: bfloat16 [1152, 1152], P('shard', 'tensor'), may hold values from -6 to 6
- momentum: float32 [1152, 1152], P('shard', 'tensor'), may hold values from -6 to 6
- damping: float32 [2], replicated, may hold values from 0.3 to 3
- coeffs: float32 [4], replicated, may hold values from 0.5 to 2
Outputs:
- new_momentum: float32 [1152, 1152], P('shard', 'tensor')
- gathered_weight: bfloat16 [1152, 1152], P(None, 'tensor')
All inputs are finite; a program needn't handle non-finite values.
Results may differ from a plain program's by a relative error of at most 0.003.
The roundings to bfloat16 on the way count: a program that leaves them out, or rounds other values in their place, can miss the bound.
Values may be sent and summed in bfloat16 or wider, within the bound.
A program may use at most 64 MiB of HBM per device.

v0:
```python
import jax
import jax.numpy as jnp
from jax import lax
from jax.sharding import PartitionSpec as P

D = 1152


def horner_columns(factor, coeffs, first_col, col_count, bound_norm):
    extent = factor.shape[0]
    row_ids = lax.broadcasted_iota(jnp.int32, (extent, col_count), 0)
    col_ids = lax.broadcasted_iota(jnp.int32, (extent, col_count), 1) + first_col
    identity_cols = (row_ids == col_ids).astype(jnp.float32)
    term_count = coeffs.shape[0]
    iterate = coeffs[term_count - 1] * identity_cols
    for term_index in range(term_count - 2, -1, -1):
        product = jnp.dot(factor, iterate.astype(jnp.bfloat16), preferred_element_type=jnp.float32)
        iterate = coeffs[term_index] * identity_cols + iterate - product / bound_norm
    return iterate


def tokens_product(left, right):
    return lax.dot_general(
        left, right, (((0,), (0,)), ((), ())), preferred_element_type=jnp.float32
    )


def on_device(acts, outgrads, weight, momentum, damping, coeffs):
    row_count = weight.shape[0]
    col_count = weight.shape[1]
    row_first = lax.axis_index("shard") * row_count
    col_first = lax.axis_index("tensor") * col_count
    full_acts, full_grads = (
        lax.all_gather(acts, "tensor", axis=1, tiled=True),
        lax.all_gather(outgrads, "tensor", axis=1, tiled=True),
    )
    local_squares = jnp.stack(
        [
            jnp.sum(jnp.square(acts.astype(jnp.float32))),
            jnp.sum(jnp.square(outgrads.astype(jnp.float32))),
        ]
    )
    traces = lax.psum(local_squares, ("shard", "tensor"))
    act_part = tokens_product(full_acts, acts)
    grad_part = tokens_product(full_grads, outgrads)
    stats = lax.psum_scatter(
        jnp.concatenate([act_part, grad_part], axis=1), "shard", scatter_dimension=0, tiled=True
    )
    row_ids = lax.broadcasted_iota(jnp.int32, (row_count, col_count), 0) + row_first
    col_ids = lax.broadcasted_iota(jnp.int32, (row_count, col_count), 1) + col_first
    diag_mask = (row_ids == col_ids).astype(jnp.float32)
    act_piece = (stats[:, :col_count] + damping[0] * traces[0] / D * diag_mask).astype(jnp.bfloat16)
    grad_piece = (stats[:, col_count:] + damping[1] * traces[1] / D * diag_mask).astype(
        jnp.bfloat16
    )
    act_wide, grad_wide = (
        lax.all_gather(act_piece, "tensor", axis=1, tiled=True),
        lax.all_gather(grad_piece, "tensor", axis=1, tiled=True),
    )
    act_full, grad_full = (
        lax.all_gather(act_wide, "shard", axis=0, tiled=True),
        lax.all_gather(grad_wide, "shard", axis=0, tiled=True),
    )
    act_scale = jnp.sqrt(jnp.sum(jnp.square(act_full.astype(jnp.float32))))
    grad_scale = jnp.sqrt(jnp.sum(jnp.square(grad_full.astype(jnp.float32))))
    act_inverse = horner_columns(act_full, coeffs, row_first, row_count, act_scale)
    grad_inverse = horner_columns(grad_full, coeffs, col_first, col_count, grad_scale).astype(
        jnp.bfloat16
    )
    projected = jnp.dot(full_grads, grad_inverse, preferred_element_type=jnp.float32).astype(
        jnp.bfloat16
    )
    right_term = tokens_product(full_acts, projected)
    right_product = lax.psum(right_term, "shard")
    update = lax.dot_general(
        act_inverse,
        right_product,
        (((0,), (0,)), ((), ())),
        precision=lax.Precision.HIGHEST,
        preferred_element_type=jnp.float32,
    )
    square_sum = lax.psum(jnp.sum(update * update), ("shard", "tensor"))
    mean_square = square_sum / (D * D)
    new_momentum = 0.9 * momentum + update / jnp.sqrt(mean_square + 1e-06)
    new_weight = (weight.astype(jnp.float32) - 0.1 * new_momentum).astype(jnp.bfloat16)
    gathered_weight = lax.all_gather(new_weight, "shard", axis=0, tiled=True)
    return (new_momentum, gathered_weight)


def solution(mesh):
    in_specs = (
        P("shard", "tensor"),
        P("shard", "tensor"),
        P("shard", "tensor"),
        P("shard", "tensor"),
        P(),
        P(),
    )
    out_specs = (P("shard", "tensor"), P(None, "tensor"))
    return jax.shard_map(
        on_device, mesh=mesh, in_specs=in_specs, out_specs=out_specs, check_vma=False
    )
```

profile of v0, /device:TPU:0, one launch (start us, length us, event | category | flops | bytes accessed | tf_op | source)
XLA Modules:
  0.0 394.1 jit_solution(14097497905494058269)
XLA Ops:
  7.2 0.0 copy-start.4
  7.2 0.0 reduce-scatter.4.cloned.1.call-start
  7.2 9.2 %all_gather.21 = bf16[256,1152]{0,1:T(8,128)(2,1)S(1)} all-gather(bf16[256,288]{0,1:T(8,128)(2,1)} %param.6), channel_id=1, replica_groups=mesh['shard'=8,'tensor'=4] {'tensor'}, dimensions={1}, use_global_device_ids=true | all-gather | bytes 737280 | tf_op jit(solution)/shard_map/all_gather | solution.py:34
  16.4 1.3 fusion.37
  17.7 0.0 copy-done.4
  17.7 7.6 %all_gather.22 = bf16[256,1152]{0,1:T(8,128)(2,1)S(1)} all-gather(bf16[256,288]{0,1:T(8,128)(2,1)S(1)} %copy-done.4), channel_id=1, replica_groups=mesh['shard'=8,'tensor'=4] {'tensor'}, dimensions={1}, use_global_device_ids=true | all-gather | bytes 737280 | tf_op jit(solution)/shard_map/all_gather | solution.py:35
  25.4 0.8 copy-done.2
  26.2 0.4 fusion.38
  26.6 0.2 pad_maximum_fusion
  26.7 2.3 copy.17
  29.1 0.0 reduce-scatter.4.cloned.1.call-update
  29.1 0.0 all-gather.7.cloned.1.call-start
  29.2 0.8 copy-done.3
  30.0 0.7 multiply_reduce_fusion.3
  30.7 0.7 multiply_reduce_fusion.2
  31.4 1.4 pad_maximum_fusion.1
  32.7 41.5 %psum.21 = f32[2]{0:T(128)S(1)} all-reduce(f32[2]{0:T(128)S(1)} %pad_maximum_fusion.1), channel_id=1, replica_groups=mesh['shard'=8,'tensor'=4] {'shard','tensor'}, use_global_device_ids=true, to_apply=%region_3.0 | all-reduce | flops 2 | bytes 16 | tf_op jit(solution)/shard_map/psum | solution.py:43
  74.2 0.6 fusion.34
  74.8 0.0 copy-done.8
  74.8 0.6 fusion.35
  78.0 25.5 %reduce-scatter.4.cloned.1.call-done = f32[144,576]{1,0:T(8,128)} async-done(((f32[1152,576]{1,0:T(8,128)}), f32[144,576]{1,0:T(8,128)}) %reduce-scatter.4.cloned.1.call-update) | async-done | bytes 331792
  103.5 1.2 fusion.33
  104.7 0.1 copy.19
  104.8 0.1 copy.20
  104.9 0.1 fusion.28
  105.1 0.1 copy.14
  105.2 6.7 %all-gather.1 = bf16[4,288,144]{1,2,0:T(8,128)(2,1)S(1)} all-gather(bf16[1,288,144]{1,2,0:T(8,128)(2,1)S(1)} %copy.14), channel_id=1, replica_groups=mesh['shard'=8,'tensor'=4] {'tensor'}, dimensions={0}, use_global_device_ids=true | all-gather | bytes 414720 | tf_op jit(solution)/shard_map/all_gather | solution.py:58
  111.9 0.2 copy.15
  112.1 1.1 reshape.13
  113.1 0.0 all-gather.7.cloned.1.call-update
  113.1 0.0 all-gather.5.cloned.1.call-start
  113.2 0.1 copy.12
  113.3 0.0 copy-start.7
  113.3 6.8 %all-gather = bf16[4,288,144]{1,2,0:T(8,128)(2,1)S(1)} all-gather(bf16[1,288,144]{1,2,0:T(8,128)(2,1)S(1)} %copy.12), channel_id=1, replica_groups=mesh['shard'=8,'tensor'=4] {'tensor'}, dimensions={0}, use_global_device_ids=true | all-gather | bytes 414720 | tf_op jit(solution)/shard_map/all_gather | solution.py:57
  120.2 0.2 copy.13
  120.3 1.1 reshape.11
  121.4 0.0 all-gather.5.cloned.1.call-update
  121.4 0.2 all-reduce.2.cloned.1.call-start
  121.6 0.0 copy-done.7
  121.7 0.7 fusion.36
  122.3 44.7 %all-gather.7.cloned.1.call-done = bf16[1152,1152]{1,0:T(8,128)(2,1)} async-done(((bf16[144,1152]{1,0:T(8,128)(2,1)}), bf16[1152,1152]{1,0:T(8,128)(2,1)}) %all-gather.7.cloned.1.call-update) | async-done | bytes 2654224 | tf_op jit(solution)/shard_map/all_gather | solution.py:62
  167.0 3.9 multiply_reduce_fusion
  171.6 0.0 copy-done.1
  171.6 2.4 fusion.2
  174.1 2.9 fusion.1
  177.0 3.9 fusion.8
  180.9 1.5 convolution_bitcast_fusion
  182.3 0.0 all-reduce.2.cloned.1.call-update
  182.3 40.7 %all-gather.5.cloned.1.call-done = bf16[1152,1152]{1,0:T(8,128)(2,1)} async-done(((bf16[144,1152]{1,0:T(8,128)(2,1)}), bf16[1152,1152]{1,0:T(8,128)(2,1)}) %all-gather.5.cloned.1.call-update) | async-done | bytes 2654224 | tf_op jit(solution)/shard_map/all_gather | solution.py:61
  223.1 3.9 multiply_reduce_fusion.1
  227.6 0.0 copy-done
  227.7 2.2 fusion.4
  229.9 1.6 fusion.5
  231.5 1.6 fusion.6
  233.1 0.0 copy-start.5
  233.1 0.0 copy-start.6
  233.1 75.8 %all-reduce.2.cloned.1.call-done = f32[1152,288]{0,1:T(8,128)} async-done(((f32[1152,288]{0,1:T(8,128)}), f32[1152,288]{0,1:T(8,128)}) %all-reduce.2.cloned.1.call-update) | async-done | bytes 1327120 | tf_op jit(solution)/shard_map/psum | solution.py:74
  308.9 3.7 multiply_reduce_fusion.4
  312.5 40.0 %psum.23 = f32[]{:T(128)} all-reduce(f32[]{:T(128)} %get-tuple-element.22), channel_id=1, replica_groups=mesh['shard'=8,'tensor'=4] {'shard','tensor'}, use_global_device_ids=true, to_apply=%region_8.0 | all-reduce | flops 1 | bytes 8 | tf_op jit(solution)/shard_map/psum | solution.py:82
  353.3 0.0 copy-done.5
  353.3 0.0 copy-done.6
  353.3 0.7 subtract_convert_fusion
  354.0 32.4 %all_gather.27 = bf16[1152,288]{1,0:T(8,128)(2,1)S(1)} all-gather(bf16[144,288]{1,0:T(8,128)(2,1)S(1)} %get-tuple-element.8), channel_id=1, replica_groups=mesh['shard'=8,'tensor'=4] {'shard'}, dimensions={0}, use_global_device_ids=true | all-gather | bytes 746496 | tf_op jit(solution)/shard_map/all_gather | solution.py:86
  386.4 1.1 copy.16
  (7 shorter events, 0.0 us)
Async XLA Ops:
  7.2 10.5 %copy-start.4 = (bf16[256,288]{0,1:T(8,128)(2,1)S(1)}, bf16[256,288]{0,1:T(8,128)(2,1)}, u32[]{:S(2)}) copy-start(bf16[256,288]{0,1:T(8,128)(2,1)} %param.7) | copy-start | bytes 442372
  7.2 96.3 %reduce-scatter.4.cloned.1.call-start = ((), (), s32[]{:S(2)}) async-start(), calls=%async_computation.4 | async-start | bytes 3317760
  25.4 0.8 copy-start.2
  29.1 0.9 copy-start.3
  29.1 45.8 %copy-start.8 = (f32[2]{0:T(128)S(1)}, f32[2]{0:T(128)}, u32[]{:S(2)}) copy-start(f32[2]{0:T(128)} %param.10) | copy-start | bytes 28
  29.1 137.9 %all-gather.7.cloned.1.call-start = ((), (), s32[]{:S(2)}) async-start(), calls=%async_computation.2 | async-start | bytes 2985984 | tf_op jit(solution)/shard_map/all_gather | solution.py:62
  113.1 110.0 %all-gather.5.cloned.1.call-start = ((), (), s32[]{:S(2)}) async-start(), calls=%async_computation.1 | async-start | bytes 2985984 | tf_op jit(solution)/shard_map/all_gather | solution.py:61
  113.3 8.3 %copy-start.7 = (f32[4]{0:T(128)S(1)}, f32[4]{0:T(128)}, u32[]{:S(2)}) copy-start(f32[4]{0:T(128)} %param.11) | copy-start | bytes 52
  121.4 187.4 %all-reduce.2.cloned.1.call-start = ((), (), s32[]{:S(2)}) async-start(), calls=%async_computation.3 | async-start | bytes 2654208 | tf_op jit(solution)/shard_map/psum | solution.py:74
  167.0 4.6 %copy-start.1 = (bf16[1152,1152]{1,0:T(8,128)(2,1)S(1)}, bf16[1152,1152]{1,0:T(8,128)(2,1)}, u32[]{:S(2)}) copy-start(bf16[1152,1152]{1,0:T(8,128)(2,1)} %all-gather.7.cloned.1.call-done) | copy-start | bytes 7962628
  223.1 4.6 %copy-start = (bf16[1152,1152]{1,0:T(8,128)(2,1)S(1)}, bf16[1152,1152]{1,0:T(8,128)(2,1)}, u32[]{:S(2)}) copy-start(bf16[1152,1152]{1,0:T(8,128)(2,1)} %all-gather.5.cloned.1.call-done) | copy-start | bytes 7962628
  233.1 120.2 %copy-start.5 = (f32[144,288]{1,0:T(8,128)S(1)}, f32[144,288]{1,0:T(8,128)}, u32[]{:S(2)}) copy-start(f32[144,288]{1,0:T(8,128)} %param.9) | copy-start | bytes 497668
  233.1 120.2 %copy-start.6 = (bf16[144,288]{1,0:T(8,128)(2,1)S(1)}, bf16[144,288]{1,0:T(8,128)(2,1)}, u32[]{:S(2)}) copy-start(bf16[144,288]{1,0:T(8,128)(2,1)} %param.8) | copy-start | bytes 248836
Sparse Core Ops, SparseCore 0:
  29.2 74.2 reduce-scatter.3
  113.2 53.7 all-gather.6
  169.4 53.5 all-gather.4
  226.9 81.9 all-reduce.1
where the time goes:
time: 395 us; the launch traced here: 394 us
  waiting for transfers between devices  187 us (47%)
  blocking collectives  144 us (36%)
  matrix products  21.4 us (5%)
  between operations  18.6 us (5%)
  other arithmetic  11.5 us (3%)
  local copies, waits for them, and re-layouts  11.1 us (3%)
    psum x1, waiting for transfers between devices, on_device(): right_product = lax.psum(right_term, 'shard')  75.8 us
    all_gather x1, waiting for transfers between devices, on_device(): lax.all_gather(grad_wide, 'shard', axis=0, tiled=True)  44.7 us
    psum x1, blocking collectives, on_device(): traces = lax.psum(local_squares, ('shard', 'tensor'))  41.5 us
    all_gather x1, waiting for transfers between devices, on_device(): lax.all_gather(act_wide, 'shard', axis=0, tiled=True)  40.7 us
    psum x1, blocking collectives, on_device(): square_sum = lax.psum(jnp.sum(update * update), ('shard', 'tensor'))  40 us
    all_gather x1, blocking collectives, on_device(): gathered_weight = lax.all_gather(new_weight, 'shard', axis=0, tiled=True)  32.4 us
    unnamed x5, waiting for transfers between devices  25.6 us
    dot_general x5, matrix products, horner_columns(): jnp.dot(factor, iterate.astype(jnp.bfloat16), preferred_element_type=jnp....  10.7 us
  transfers between devices with their start and end apart: 4, of which 4 were waited for; matrix products, arithmetic and copies ran while one was open for 8% of the time, Pallas kernels for 0%

commit v1 on v0

--- a/solution.py
+++ b/solution.py
@@ -59,7 +59,9 @@
     )
     act_full, grad_full = (
         lax.all_gather(act_wide, "shard", axis=0, tiled=True),
-        lax.all_gather(grad_wide, "shard", axis=0, tiled=True),
+        jnp.concatenate(
+            lax.all_to_all(jnp.stack([grad_wide] * lax.axis_size("shard")), "shard", 0, 0), axis=0
+        ),
     )
     act_scale = jnp.sqrt(jnp.sum(jnp.square(act_full.astype(jnp.float32))))
     grad_scale = jnp.sqrt(jnp.sum(jnp.square(grad_full.astype(jnp.float32))))

time: 395 us -> 386 us (0.977)
  waiting for transfers between devices: 187 us -> 172 us
    all_to_all x0 -> x1, waiting for transfers between devices: none -> 75 us  [on_device(): lax.all_to_all(jnp.stack([grad_wide] * lax.axis_size('shard')), 'shard',...]
    all_gather x1 -> x0, waiting for transfers between devices: 44.7 us -> none  [on_device(): lax.all_gather(grad_wide, 'shard', axis=0, tiled=True)]
    all_gather x1, waiting for transfers between devices: 40.7 us -> 0.02 us  [on_device(): lax.all_gather(act_wide, 'shard', axis=0, tiled=True)]
    psum x1, waiting for transfers between devices: 75.8 us -> 71.1 us  [on_device(): right_product = lax.psum(right_term, 'shard')]
    unnamed x5 -> x4, waiting for transfers between devices: 25.6 us -> 26.1 us
    unnamed x26 -> x24, local copies, waits for them, and re-layouts: 7.78 us -> 8.15 us
  transfers between devices with their start and end apart: 4 -> 4, of which waited for: 4 -> 3; matrix products, arithmetic and copies ran while one was open for 8% -> 8% of each run, Pallas kernels for 0% -> 0%
where the time goes in v1:
time: 386 us; the launch traced here: 385 us
  waiting for transfers between devices  172 us (45%)
  blocking collectives  144 us (37%)
  matrix products  22.4 us (6%)
  between operations  18.5 us (5%)
  local copies, waits for them, and re-layouts  14 us (4%)
  other arithmetic  9.51 us (2%)
  starting transfers between devices  4.03 us (1%)
    all_to_all x1, waiting for transfers between devices, on_device(): lax.all_to_all(jnp.stack([grad_wide] * lax.axis_size('shard')), 'shard',...  75 us
    psum x1, waiting for transfers between devices, on_device(): right_product = lax.psum(right_term, 'shard')  71.1 us
    psum x1, blocking collectives, on_device(): traces = lax.psum(local_squares, ('shard', 'tensor'))  41.6 us
    psum x1, blocking collectives, on_device(): square_sum = lax.psum(jnp.sum(update * update), ('shard', 'tensor'))  40.1 us
    all_gather x1, blocking collectives, on_device(): gathered_weight = lax.all_gather(new_weight, 'shard', axis=0, tiled=True)  32.4 us
    unnamed x4, waiting for transfers between devices  26.1 us
    dot_general x5, matrix products, horner_columns(): jnp.dot(factor, iterate.astype(jnp.bfloat16), preferred_element_type=jnp....  11.5 us
    all_gather x1, blocking collectives, on_device(): lax.all_gather(acts, 'tensor', axis=1, tiled=True)  9.19 us
  transfers between devices with their start and end apart: 4, of which 3 were waited for; matrix products, arithmetic and copies ran while one was open for 8% of the time, Pallas kernels for 0%

profile of v1, /device:TPU:0, one launch (start us, length us, event | category | flops | bytes accessed | tf_op | source)
XLA Modules:
  0.0 385.0 jit_solution(11950317847489809245)
XLA Ops:
  7.2 0.0 copy-start.3
  7.2 0.0 reduce-scatter.4.cloned.1.call-start
  7.2 9.2 %all_gather.18 = bf16[256,1152]{0,1:T(8,128)(2,1)S(1)} all-gather(bf16[256,288]{0,1:T(8,128)(2,1)} %param.6), channel_id=1, replica_groups=mesh['shard'=8,'tensor'=4] {'tensor'}, dimensions={1}, use_global_device_ids=true | all-gather | bytes 737280 | tf_op jit(solution)/shard_map/all_gather | solution.py:34
  16.4 1.3 fusion.37
  17.7 0.0 copy-done.3
  17.7 7.6 %all_gather.19 = bf16[256,1152]{0,1:T(8,128)(2,1)S(1)} all-gather(bf16[256,288]{0,1:T(8,128)(2,1)S(1)} %copy-done.3), channel_id=1, replica_groups=mesh['shard'=8,'tensor'=4] {'tensor'}, dimensions={1}, use_global_device_ids=true | all-gather | bytes 737280 | tf_op jit(solution)/shard_map/all_gather | solution.py:35
  25.4 0.0 copy-start.1
  25.4 0.8 copy-done.1
  26.2 0.4 fusion.38
  26.6 0.2 pad_maximum_fusion
  26.7 2.3 copy.24
  29.1 0.0 copy-start.2
  29.1 0.0 reduce-scatter.4.cloned.1.call-update
  29.1 0.9 copy-done.2
  30.0 0.7 multiply_reduce_fusion.3
  30.7 0.7 multiply_reduce_fusion.2
  31.3 1.3 pad_maximum_fusion.1
  32.6 41.6 %psum.21 = f32[2]{0:T(128)S(1)} all-reduce(f32[2]{0:T(128)S(1)} %pad_maximum_fusion.1), channel_id=1, replica_groups=mesh['shard'=8,'tensor'=4] {'shard','tensor'}, use_global_device_ids=true, to_apply=%region_3.0 | all-reduce | flops 2 | bytes 16 | tf_op jit(solution)/shard_map/psum | solution.py:43
  74.3 0.6 fusion.34
  74.9 0.0 copy-done.7
  74.9 0.6 fusion.35
  78.0 26.1 %reduce-scatter.4.cloned.1.call-done = f32[144,576]{1,0:T(8,128)} async-done(((f32[1152,576]{1,0:T(8,128)}), f32[144,576]{1,0:T(8,128)}) %reduce-scatter.4.cloned.1.call-update) | async-done | bytes 331792
  104.1 1.2 fusion.33
  105.2 0.1 copy.26
  105.4 0.1 copy.27
  105.5 0.1 fusion.28
  105.7 0.1 copy.21
  105.8 6.7 %all-gather.1 = bf16[4,288,144]{1,2,0:T(8,128)(2,1)S(1)} all-gather(bf16[1,288,144]{1,2,0:T(8,128)(2,1)S(1)} %copy.21), channel_id=1, replica_groups=mesh['shard'=8,'tensor'=4] {'tensor'}, dimensions={0}, use_global_device_ids=true | all-gather | bytes 414720 | tf_op jit(solution)/shard_map/all_gather | solution.py:58
  112.5 0.2 copy.22
  112.6 0.3 reshape.19
  113.0 1.7 stack.11
  114.7 3.7 all-to-all-start
  118.4 0.0 all-gather.4.cloned.1.call-start
  118.4 0.1 copy.19
  118.6 0.0 copy-start.6
  118.6 6.8 %all-gather = bf16[4,288,144]{1,2,0:T(8,128)(2,1)S(1)} all-gather(bf16[1,288,144]{1,2,0:T(8,128)(2,1)S(1)} %copy.19), channel_id=1, replica_groups=mesh['shard'=8,'tensor'=4] {'tensor'}, dimensions={0}, use_global_device_ids=true | all-gather | bytes 414720 | tf_op jit(solution)/shard_map/all_gather | solution.py:57
  125.3 0.9 copy.20
  126.3 2.1 reshape.17
  128.4 0.0 all-gather.4.cloned.1.call-update
  128.4 0.2 all-reduce.2.cloned.1.call-start
  128.7 0.0 copy-done.6
  128.7 0.7 fusion.36
  129.3 75.0 %all-to-all-done = bf16[8,144,1152]{2,1,0:T(8,128)(2,1)S(1)} async-done(((bf16[8,144,1152]{2,1,0:T(8,128)(2,1)}), bf16[8,144,1152]{2,1,0:T(8,128)(2,1)S(1)}, u32[]{:S(2)}, u32[]{:S(2)}) %all-to-all-start) | async-done | bytes 2654240 | tf_op jit(solution)/shard_map/all_to_all | solution.py:63
  204.3 2.0 multiply_reduce_fusion
  206.9 2.4 fusion.2
  209.3 3.0 fusion.1
  212.3 3.8 fusion.8
  216.1 1.5 convolution_bitcast_fusion
  217.6 0.0 all-reduce.2.cloned.1.call-update
  217.6 0.0 all-gather.4.cloned.1.call-done
  217.6 0.0 copy-start
  217.7 3.9 %multiply_reduce_fusion.1 = f32[]{:T(128)} fusion(bf16[1152,1152]{1,0:T(8,128)(2,1)} %all-gather.4.cloned.1.call-done), kind=kLoop, calls=%fused_computation.1 | loop fusion | flops 3981311 | bytes 2654212 | tf_op jit(solution)/shard_map/reduce_sum | solution.py:66
  222.2 0.0 copy-done
  222.2 2.2 fusion.4
  224.4 1.7 fusion.5
  226.1 2.4 fusion.6
  228.4 71.1 %all-reduce.2.cloned.1.call-done = f32[1152,288]{0,1:T(8,128)} async-done(((f32[1152,288]{0,1:T(8,128)}), f32[1152,288]{0,1:T(8,128)}) %all-reduce.2.cloned.1.call-update) | async-done | bytes 1327120 | tf_op jit(solution)/shard_map/psum | solution.py:76
  299.5 3.9 %multiply_reduce_fusion.4 = (f32[]{:T(128)}, f32[144,288]{1,0:T(8,128)S(1)}) fusion(f32[1152,144]{0,1:T(8,128)} %fusion.6, f32[1152,288]{0,1:T(8,128)} %all-reduce.2.cloned.1.call-done), kind=kOutput, calls=%fused_computation.49 | convolution fusion | flops 573391872 | bytes 2156548 | tf_op jit(solution)/shard_map/dot_general | solution.py:77
  303.4 40.1 %psum.23 = f32[]{:T(128)} all-reduce(f32[]{:T(128)} %get-tuple-element.24), channel_id=1, replica_groups=mesh['shard'=8,'tensor'=4] {'shard','tensor'}, use_global_device_ids=true, to_apply=%region_8.0 | all-reduce | flops 1 | bytes 8 | tf_op jit(solution)/shard_map/psum | solution.py:84
  344.1 0.0 copy-done.4
  344.2 0.0 copy-done.5
  344.2 0.8 subtract_convert_fusion
  344.9 32.4 %all_gather.23 = bf16[1152,288]{1,0:T(8,128)(2,1)S(1)} all-gather(bf16[144,288]{1,0:T(8,128)(2,1)S(1)} %get-tuple-element.10), channel_id=1, replica_groups=mesh['shard'=8,'tensor'=4] {'shard'}, dimensions={0}, use_global_device_ids=true | all-gather | bytes 746496 | tf_op jit(solution)/shard_map/all_gather | solution.py:88
  377.3 1.1 copy.23
  (5 shorter events, 0.0 us)
Async XLA Ops:
  7.2 10.5 %copy-start.3 = (bf16[256,288]{0,1:T(8,128)(2,1)S(1)}, bf16[256,288]{0,1:T(8,128)(2,1)}, u32[]{:S(2)}) copy-start(bf16[256,288]{0,1:T(8,128)(2,1)} %param.7) | copy-start | bytes 442372
  7.2 96.9 %reduce-scatter.4.cloned.1.call-start = ((), (), s32[]{:S(2)}) async-start(), calls=%async_computation.4 | async-start | bytes 3317760
  25.4 0.8 copy-start.1
  29.1 0.9 copy-start.2
  29.1 45.8 %copy-start.7 = (f32[2]{0:T(128)S(1)}, f32[2]{0:T(128)}, u32[]{:S(2)}) copy-start(f32[2]{0:T(128)} %param.10) | copy-start | bytes 28
  114.7 89.6 %all-to-all-start = ((bf16[8,144,1152]{2,1,0:T(8,128)(2,1)}), bf16[8,144,1152]{2,1,0:T(8,128)(2,1)S(1)}, u32[]{:S(2)}, u32[]{:S(2)}) async-start(bf16[8,144,1152]{2,1,0:T(8,128)(2,1)} %stack.11), calls=%async_computation | async-start | bytes 5308416 | tf_op jit(solution)/shard_map/all_to_all | solution.py:63
  118.4 99.2 %all-gather.4.cloned.1.call-start = ((), (), s32[]{:S(2)}) async-start(), calls=%async_computation.2 | async-start | bytes 2985984 | tf_op jit(solution)/shard_map/all_gather | solution.py:61
  118.6 10.1 %copy-start.6 = (f32[4]{0:T(128)S(1)}, f32[4]{0:T(128)}, u32[]{:S(2)}) copy-start(f32[4]{0:T(128)} %param.11) | copy-start | bytes 52
  128.4 171.1 %all-reduce.2.cloned.1.call-start = ((), (), s32[]{:S(2)}) async-start(), calls=%async_computation.3 | async-start | bytes 2654208 | tf_op jit(solution)/shard_map/psum | solution.py:76
  217.6 4.6 %copy-start = (bf16[1152,1152]{1,0:T(8,128)(2,1)S(1)}, bf16[1152,1152]{1,0:T(8,128)(2,1)}, u32[]{:S(2)}) copy-start(bf16[1152,1152]{1,0:T(8,128)(2,1)} %all-gather.4.cloned.1.call-done) | copy-start | bytes 7962628
  228.4 115.7 %copy-start.4 = (f32[144,288]{1,0:T(8,128)S(1)}, f32[144,288]{1,0:T(8,128)}, u32[]{:S(2)}) copy-start(f32[144,288]{1,0:T(8,128)} %param.9) | copy-start | bytes 497668
  228.4 115.7 %copy-start.5 = (bf16[144,288]{1,0:T(8,128)(2,1)S(1)}, bf16[144,288]{1,0:T(8,128)(2,1)}, u32[]{:S(2)}) copy-start(bf16[144,288]{1,0:T(8,128)(2,1)} %param.8) | copy-start | bytes 248836
Sparse Core Ops, SparseCore 0:
  29.2 74.8 reduce-scatter.3
  128.5 83.1 all-gather.3
  217.7 81.7 all-reduce.1
